TPU v7x, 32 devices: a whole 2x2x4 slice. The times are simulated.
32 devices in a mesh: grp: 2 (over y), seq: 4 (over z), head: 2 (over x), sub: 2 (over core).
Axes of the slice: x: 2, y: 2, z: 4, core: 2. Of those that a mesh axis runs over, the one named last changes fastest.
Arguments:
- queries: float32 [1536, 2048], P(('grp', 'seq'), ('head', 'sub')), parts along dimension 0, may hold values from -6 to 6
- keys: float32 [1536, 2048], P(('grp', 'seq'), ('head', 'sub')), parts along dimension 0, may hold values from -6 to 6
- values: float32 [1536, 2048], P(('grp', 'seq'), ('head', 'sub')), parts along dimension 0, may hold values from -40 to 40
- opt_queries: float32 [16, 64, 2048], P(('grp', 'seq'), None, ('head', 'sub')), parts along dimension 0, may hold values from -6 to 6
- opt_keys: float32 [16, 64, 2048], P(('grp', 'seq'), None, ('head', 'sub')), parts along dimension 0, may hold values from -6 to 6
- opt_values: float32 [16, 64, 2048], P(('grp', 'seq'), None, ('head', 'sub')), parts along dimension 0, may hold values from -40 to 40
- opt_offsets: int32 [16], P(('grp', 'seq')), parts along dimension 0, may hold values from 0 to 192
- opt_lengths: int32 [16], P(('grp', 'seq')), parts along dimension 0, may hold values from 1 to 64, 320 in all
- norm_gain: float32 [2048], P(('head', 'sub')), may hold values from 0.5 to 2
- out_weight: bfloat16 [2048, 4096], P(('head', 'sub')), may hold values from -0.125 to 0.125
Outputs:
- ctx_out: bfloat16 [1536, 4096], P(('grp', 'seq'), ('head', 'sub')), parts along dimension 0
- opt_out: bfloat16 [16, 64, 4096], P(('grp', 'seq'), None, ('head', 'sub')), parts along dimension 0
There are 2 independent parts, one for each index of `grp`. A program takes and returns all parts, laid end to end along the dimension named above; an argument that names none is the same for every part. Nothing has to cross between parts.
Inputs may be any that keep to these rules, and one draw needn't show every extreme that they name: `opt_lengths`: within each scoring group the 8 lengths sum to 320, and the longest option of each group has exactly 64 tokens in every draw.
All inputs are finite; a program needn't handle non-finite values.
Results may differ from a plain program's by a relative error of at most 0.017.
Values may be sent and summed in bfloat16 or wider, within the bound.
A program may use at most 64 MiB of HBM per device.

v0:
```python
import jax
import jax.numpy as jnp
from jax import lax
from jax.sharding import PartitionSpec as P

DH = 128
norm_epsilon = 1e-05


def entering(value, axis, join, neutral):
    place = lax.axis_index(axis)
    gathered = lax.all_gather(value.astype(jnp.bfloat16), axis)
    state = jnp.zeros_like(value) + jnp.asarray(neutral, value.dtype)

    def one(hop, state):
        return join(state, lax.dynamic_index_in_dim(gathered, hop, 0, False).astype(value.dtype))

    return lax.fori_loop(0, place, one, state)


def head_norm(attended, gain, mask):
    mean_square = jnp.mean(attended * attended, axis=-1, keepdims=True)
    return (attended * lax.rsqrt(mean_square + norm_epsilon) * gain * mask).astype(jnp.bfloat16)


def combine_sum(earlier, later):
    return earlier + later


def grouped_project(rows, weight_columns, groups):
    count = rows.shape[0]
    flat = rows.reshape(count, groups, rows.shape[1] // groups)
    weight_groups = weight_columns.reshape(
        groups, weight_columns.shape[0] // groups, weight_columns.shape[1]
    )
    partial_value = jnp.einsum(
        "rgk,gkd->grd", flat, weight_groups, preferred_element_type=jnp.float32
    )
    partial_value = lax.optimization_barrier(partial_value.astype(jnp.bfloat16)).astype(jnp.float32)
    return jnp.sum(partial_value, axis=0).astype(jnp.bfloat16)


def on_device(
    queries,
    keys,
    values,
    opt_queries,
    opt_keys,
    opt_values,
    opt_offsets,
    opt_lengths,
    norm_gain,
    out_weight,
):
    highest = lax.Precision.HIGHEST
    tok_rows = queries.shape[0]
    heads = queries.shape[1] // DH
    opt_count = opt_queries.shape[0]
    slot_count = opt_queries.shape[1]
    group_count = lax.axis_size(("head", "sub"))
    weight_columns = lax.all_to_all(
        out_weight, ("head", "sub"), split_axis=1, concat_axis=0, tiled=True
    )
    block_q = queries.reshape(tok_rows, heads, DH)
    block_k = keys.reshape(tok_rows, heads, DH)
    block_v = values.reshape(tok_rows, heads, DH)
    gain = norm_gain.reshape(heads, DH)
    states = jnp.einsum("thd,the->hde", block_k, block_v, precision=highest)
    positions = jnp.arange(tok_rows, dtype=jnp.int32)
    causal = (positions[:, None] >= positions[None, :]).astype(jnp.float32)
    scores = jnp.einsum("thd,shd->hts", block_q, block_k, precision=highest) * causal[None]
    intra = jnp.einsum("hts,she->the", scores, block_v, precision=highest)
    opt_q = opt_queries.reshape(opt_count, slot_count, heads, DH)
    opt_k = opt_keys.reshape(opt_count, slot_count, heads, DH)
    opt_v = opt_values.reshape(opt_count, slot_count, heads, DH)
    before = (positions[None, :] < opt_offsets[:, None]).astype(jnp.float32)
    local = jnp.einsum("ot,thd,the->ohde", before, block_k, block_v, precision=highest)
    slots = jnp.arange(slot_count, dtype=jnp.int32)
    slot_causal = (slots[:, None] >= slots[None, :]).astype(jnp.float32)
    opt_scores = (
        jnp.einsum("oihd,ojhd->ohij", opt_q, opt_k, precision=highest) * slot_causal[None, None]
    )
    opt_intra = jnp.einsum("ohij,ojhe->oihe", opt_scores, opt_v, precision=highest)
    prefix = entering(states, "seq", combine_sum, jnp.zeros_like(states))
    inter = jnp.einsum("thd,hde->the", block_q, prefix, precision=highest)
    context_normed = head_norm(inter + intra, gain, 1.0).reshape(tok_rows, heads * DH)
    opt_state = prefix[None] + local
    opt_inter = jnp.einsum("oihd,ohde->oihe", opt_q, opt_state, precision=highest)
    valid = (slots[None, :] < opt_lengths[:, None]).astype(jnp.float32)
    opt_normed = head_norm(opt_inter + opt_intra, gain, valid[:, :, None, None]).reshape(
        opt_count * slot_count, heads * DH
    )
    gathered_ctx, gathered_opt = (
        lax.all_gather(context_normed, ("head", "sub"), axis=1, tiled=True),
        lax.all_gather(opt_normed, ("head", "sub"), axis=1, tiled=True),
    )
    context_out = grouped_project(gathered_ctx, weight_columns, group_count)
    opt_rows = grouped_project(gathered_opt, weight_columns, group_count)
    option_out = opt_rows.reshape(opt_count, slot_count, opt_rows.shape[1])
    return (context_out, option_out)


def solution(mesh):
    placed = (
        P(("grp", "seq"), ("head", "sub")),
        P(("grp", "seq"), ("head", "sub")),
        P(("grp", "seq"), ("head", "sub")),
        P(("grp", "seq"), None, ("head", "sub")),
        P(("grp", "seq"), None, ("head", "sub")),
        P(("grp", "seq"), None, ("head", "sub")),
        P(("grp", "seq")),
        P(("grp", "seq")),
        P(("head", "sub")),
        P(("head", "sub"), None),
    )
    return jax.shard_map(
        on_device,
        mesh=mesh,
        in_specs=placed,
        out_specs=(P(("grp", "seq"), ("head", "sub")), P(("grp", "seq"), None, ("head", "sub"))),
        check_vma=False,
    )
```

profile of v0, /device:TPU:0, one launch (start us, length us, event | category | flops | bytes accessed | tf_op | source)
XLA Modules:
  0.0 91.5 jit_solution(10964770409362976219)
XLA Ops:
  0.6 6.5 %copy.40 = bf16[512,4096]{0,1:T(8,128)(2,1)} copy(bf16[512,4096]{1,0:T(8,128)(2,1)} %param.21) | data formatting | bytes 8388608 | tf_op args[9]
  7.2 6.3 %copy.41 = bf16[512,4,1024]{2,0,1:T(8,128)(2,1)} copy(bf16[512,4,1024]{0,2,1:T(8,128)(2,1)} %bitcast.132) | data formatting | bytes 8388608 | tf_op jit(solution)/shard_map/all_to_all | solution.py:61
  13.5 5.0 %all-to-all-start = ((bf16[512,4,1024]{2,0,1:T(8,128)(2,1)}), bf16[512,4,1024]{2,0,1:T(8,128)(2,1)}, u32[]{:S(2)}, u32[]{:S(2)}) async-start(bf16[512,4,1024]{2,0,1:T(8,128)(2,1)} %copy.41), calls=%async_computation | async-start | bytes 8388608 | tf_op jit(solution)/shard_map/all_to_all | solution.py:61
  18.6 1.1 %convolution_convert_fusion = bf16[4,128,128]{2,1,0:T(8,128)(2,1)S(1)} fusion(f32[192,512]{1,0:T(8,128)S(1)} %copy-done.1, f32[192,512]{1,0:T(8,128)S(1)} %copy-done), kind=kOutput, calls=%fused_computation.17 | convolution fusion | flops 151060480 | bytes 917504 | tf_op jit(solution)/shard_map/thd,the->hde/dot_general | solution.py:68
  19.7 17.9 %all-gather = bf16[16,128,128]{2,1,0:T(8,128)(2,1)S(1)} all-gather(bf16[4,128,128]{2,1,0:T(8,128)(2,1)S(1)} %convolution_convert_fusion), channel_id=2, replica_groups=mesh['grp'=2,'seq'=4,'head'=2,'sub'=2] {'seq'}, dimensions={0}, use_global_device_ids=true | all-gather | bytes 655360 | tf_op jit(solution)/shard_map/all_gather | solution.py:12
  37.6 0.1 fusion.39
  37.7 0.5 convolution_multiply_fusion.1
  38.3 0.1 compare_convert_fusion.1
  38.4 1.9 %fusion.10 = f32[2,4,128,128]{3,2,1,0:T(8,128)S(1)} fusion(f32[192,4,128]{2,0,1:T(8,128)S(1)} %copy_bitcast_fusion, f32[192,2]{0,1:T(2,128)S(1)} %fusion.39, f32[4,128,128]{2,1,0:T(8,128)S(1)} %get-tuple-element.25, f32[192,512]{1,0:T(8,128)S(1)} %copy-done.1), kind=kOutput, calls=%fused_computation.9 | convolution fusion | flops 302317568 | bytes 1574400 | tf_op jit(solution)/shard_map/ot,thd,the->ohde/dot_general | solution.py:77
  40.3 0.6 convolution_bitcast_fusion.3
  40.9 0.5 multiply_reduce_fusion.1
  41.4 0.2 multiply_convert_fusion.1
  41.6 0.1 copy.49
  41.7 29.2 %all_gather.15 = bf16[128,2048]{1,0:T(8,128)(2,1)S(1)} all-gather(bf16[128,512]{1,0:T(8,128)(2,1)S(1)} %bitcast.136), channel_id=1, replica_groups=mesh['grp'=2,'seq'=4,'head'=2,'sub'=2] {'head','sub'}, dimensions={1}, use_global_device_ids=true | all-gather | bytes 655360 | tf_op jit(solution)/shard_map/all_gather | solution.py:95
  70.9 1.0 %copy.50 = bf16[128,2048]{0,1:T(8,128)(2,1)} copy(bf16[128,2048]{1,0:T(8,128)(2,1)S(1)} %all_gather.15) | data formatting | bytes 1048576 | tf_op jit(solution)/shard_map/all_gather | solution.py:95
  72.0 0.5 convolution_bitcast_fusion.1
  72.5 0.8 convolution_multiply_fusion
  73.3 1.0 %multiply_reduce_fusion = (f32[192,4]{0,1:T(4,128)S(1)}, f32[192,4,128]{2,0,1:T(8,128)S(1)}) fusion(f32[192,4,128]{2,0,1:T(8,128)S(1)} %convolution_bitcast_fusion.1, f32[4,192,192]{2,1,0:T(8,128)S(1)} %convolution_multiply_fusion, f32[192,512]{1,0:T(8,128)S(1)} %copy-done.1), kind=kOutput, calls=%fused_computation.31 | convolution fusion | flops 226786560 | bytes 1772544 | tf_op jit(solution)/shard_map/hts,she->the/dot_general | solution.py:72
  74.3 0.2 copy_bitcast_fusion.1
  74.5 8.7 %all_gather.14 = bf16[192,2048]{1,0:T(8,128)(2,1)S(1)} all-gather(bf16[192,512]{1,0:T(8,128)(2,1)S(1)} %copy_bitcast_fusion.1), channel_id=1, replica_groups=mesh['grp'=2,'seq'=4,'head'=2,'sub'=2] {'head','sub'}, dimensions={1}, use_global_device_ids=true | all-gather | bytes 983040 | tf_op jit(solution)/shard_map/all_gather | solution.py:94
  83.2 3.2 %fusion.4 = bf16[4,192,1024]{2,1,0:T(8,128)(2,1)S(1)} fusion(bf16[512,4,1024]{2,0,1:T(8,128)(2,1)} %all-to-all-done, bf16[24,4,8,512]{3,2,1,0:T(8,128)(2,1)S(1)} %bitcast.133), kind=kOutput, calls=%fused_computation.5 | convolution fusion | flops 806092800 | bytes 6553600 | tf_op jit(solution)/shard_map/rgk,gkd->grd/dot_general | solution.py:36
  86.4 3.0 %fusion.7 = bf16[4,128,1024]{2,1,0:T(8,128)(2,1)S(1)} fusion(bf16[128,4,512]{0,2,1:T(8,128)(2,1)S(1)} %bitcast.134, bf16[512,4,1024]{2,0,1:T(8,128)(2,1)} %all-to-all-done), kind=kOutput, calls=%fused_computation.6 | convolution fusion | flops 537395200 | bytes 5767168 | tf_op jit(solution)/shard_map/rgk,gkd->grd/dot_general | solution.py:36
  89.4 1.1 %reduce_sum.43 = bf16[192,1024]{1,0:T(8,128)(2,1)} reduce(bf16[4,192,1024]{2,1,0:T(8,128)(2,1)S(1)} %fusion.4, bf16[]{:T(256)} %constant.28.clone.1), dimensions={0}, to_apply=%region_3.4 | reduce | flops 589824 | bytes 1966082 | tf_op jit(solution)/shard_map/reduce_sum | solution.py:40
  90.6 0.9 %reduce_sum.45 = bf16[128,1024]{1,0:T(8,128)(2,1)} reduce(bf16[4,128,1024]{2,1,0:T(8,128)(2,1)S(1)} %fusion.7, bf16[]{:T(256)} %constant.28.clone.1), dimensions={0}, to_apply=%region_5.6 | reduce | flops 393216 | bytes 1310722 | tf_op jit(solution)/shard_map/reduce_sum | solution.py:40
  (29 shorter events, 0.2 us)
Async XLA Ops:
  0.6 17.9 %copy-start = (f32[192,512]{1,0:T(8,128)S(1)}, f32[192,512]{1,0:T(8,128)}, u32[]{:S(2)}) copy-start(f32[192,512]{1,0:T(8,128)} %param.13) | copy-start | bytes 1179652
  13.5 5.1 %copy-start.1 = (f32[192,512]{1,0:T(8,128)S(1)}, f32[192,512]{1,0:T(8,128)}, u32[]{:S(2)}) copy-start(f32[192,512]{1,0:T(8,128)} %param.14) | copy-start | bytes 1179652
  13.5 69.7 %all-to-all-start = ((bf16[512,4,1024]{2,0,1:T(8,128)(2,1)}), bf16[512,4,1024]{2,0,1:T(8,128)(2,1)}, u32[]{:S(2)}, u32[]{:S(2)}) async-start(bf16[512,4,1024]{2,0,1:T(8,128)(2,1)} %copy.41), calls=%async_computation | async-start | bytes 8388608 | tf_op jit(solution)/shard_map/all_to_all | solution.py:61
  18.5 19.1 %copy-start.8 = (s32[2]{0:T(128)S(1)}, s32[2]{0:T(128)}, u32[]{:S(2)}) copy-start(s32[2]{0:T(128)} %param.18) | copy-start | bytes 28
  18.5 19.2 %copy-start.4 = (f32[2,64,512]{2,1,0:T(8,128)S(1)}, f32[2,64,512]{2,1,0:T(8,128)}, u32[]{:S(2)}) copy-start(f32[2,64,512]{2,1,0:T(8,128)} %param.15) | copy-start | bytes 786436
  18.5 19.2 %copy-start.5 = (f32[2,64,512]{2,1,0:T(8,128)S(1)}, f32[2,64,512]{2,1,0:T(8,128)}, u32[]{:S(2)}) copy-start(f32[2,64,512]{2,1,0:T(8,128)} %param.16) | copy-start | bytes 786436
  18.5 19.8 %copy-start.9 = (s32[2]{0:T(128)S(1)}, s32[2]{0:T(128)}, u32[]{:S(2)}) copy-start(s32[2]{0:T(128)} %param.19) | copy-start | bytes 28
  18.6 22.2 %copy-start.6 = (f32[2,64,512]{2,1,0:T(8,128)S(1)}, f32[2,64,512]{2,1,0:T(8,128)}, u32[]{:S(2)}) copy-start(f32[2,64,512]{2,1,0:T(8,128)} %param.17) | copy-start | bytes 786436
  37.6 3.8 %copy-start.7 = (f32[512]{0:T(512)S(1)}, f32[512]{0:T(512)}, u32[]{:S(2)}) copy-start(f32[512]{0:T(512)} %param.20) | copy-start | bytes 6148
  37.6 34.4 %copy-start.3 = (f32[192,512]{1,0:T(8,128)S(1)}, f32[192,512]{1,0:T(8,128)}, u32[]{:S(2)}) copy-start(f32[192,512]{1,0:T(8,128)} %param.12) | copy-start | bytes 1179652
  83.2 3.2 %copy-start.2 = (bf16[128,2048]{0,1:T(8,128)(2,1)S(1)}, bf16[128,2048]{0,1:T(8,128)(2,1)}, u32[]{:S(2)}) copy-start(bf16[128,2048]{0,1:T(8,128)(2,1)} %copy.50) | copy-start | bytes 1572868
where the time goes:
time: 92 us; the launch traced here: 91.5 us
  blocking collectives  55.8 us (61%)
  local copies, waits for them, and re-layouts  14.1 us (15%)
  matrix products  13.1 us (14%)
  starting transfers between devices  4.97 us (5%)
  other arithmetic  2.58 us (3%)
    all_gather x1, blocking collectives, on_device(): lax.all_gather(opt_normed, ('head', 'sub'), axis=1, tiled=True)  29.2 us
    all_gather x1, blocking collectives, entering(): gathered = lax.all_gather(value.astype(jnp.bfloat16), axis)  17.9 us
    all_gather x1, blocking collectives, on_device(): lax.all_gather(context_normed, ('head', 'sub'), axis=1, tiled=True)  8.71 us
    unnamed x22, local copies, waits for them, and re-layouts  6.62 us
    all_to_all x1, local copies, waits for them, and re-layouts, on_device(): lax.all_to_all(out_weight, ('head', 'sub'), split_axis=1, concat_axis=0,...  6.33 us
    dot_general x2, matrix products, grouped_project(): jnp.einsum('rgk,gkd->grd', flat, weight_groups, preferred_element_type=jn...  6.22 us
    all_to_all x1, starting transfers between devices, on_device(): lax.all_to_all(out_weight, ('head', 'sub'), split_axis=1, concat_axis=0,...  4.97 us
    reduce_sum x2, other arithmetic, grouped_project(): return jnp.sum(partial_value, axis=0).astype(jnp.bfloat16)  2.06 us
  transfers between devices with their start and end apart: 1, of which 0 were waited for; matrix products, arithmetic and copies ran while one was open for 9% of the time, Pallas kernels for 0%

commit v1 on v0

--- a/solution.py
+++ b/solution.py
@@ -58,8 +58,14 @@
     opt_count = opt_queries.shape[0]
     slot_count = opt_queries.shape[1]
     group_count = lax.axis_size(("head", "sub"))
-    weight_columns = lax.all_to_all(
-        out_weight, ("head", "sub"), split_axis=1, concat_axis=0, tiled=True
+    weight_columns = jnp.concatenate(
+        lax.all_to_all(
+            jnp.stack(jnp.split(out_weight, lax.axis_size(("head", "sub")), axis=1)),
+            ("head", "sub"),
+            0,
+            0,
+        ),
+        axis=0,
     )
     block_q = queries.reshape(tok_rows, heads, DH)
     block_k = keys.reshape(tok_rows, heads, DH)

time: 92 us -> 83.5 us (0.908)
  local copies, waits for them, and re-layouts: 14.1 us -> 3.18 us
  other arithmetic: 2.58 us -> 4.85 us
    unnamed x22 -> x21, local copies, waits for them, and re-layouts: 6.62 us -> 0.08 us
    all_to_all x1 -> x0, local copies, waits for them, and re-layouts: 6.33 us -> none  [on_device(): lax.all_to_all(out_weight, ('head', 'sub'), split_axis=1, concat_axis=0,...]
    another operation x0 -> x1, local copies, waits for them, and re-layouts: none -> 2.68 us  [on_device(): jnp.stack(jnp.split(out_weight, lax.axis_size(('head', 'sub')), axis=1))]
    another operation x1 -> x2, other arithmetic: 0.07 us -> 2.34 us  [the longest x1 2.27 us: on_device(): jnp.stack(jnp.split(out_weight, lax.axis_size(('head', 'sub')), axis=1))]
where the time goes in v1:
time: 83.5 us; the launch traced here: 83.3 us
  blocking collectives  56.3 us (67%)
  matrix products  13.1 us (16%)
  starting transfers between devices  4.96 us (6%)
  other arithmetic  4.85 us (6%)
  local copies, waits for them, and re-layouts  3.18 us (4%)
  between operations  0.91 us (1%)
    all_gather x1, blocking collectives, on_device(): lax.all_gather(opt_normed, ('head', 'sub'), axis=1, tiled=True)  29.2 us
    all_gather x1, blocking collectives, entering(): gathered = lax.all_gather(value.astype(jnp.bfloat16), axis)  17.9 us
    all_gather x1, blocking collectives, on_device(): lax.all_gather(context_normed, ('head', 'sub'), axis=1, tiled=True)  9.16 us
    dot_general x2, matrix products, grouped_project(): jnp.einsum('rgk,gkd->grd', flat, weight_groups, preferred_element_type=jn...  6.23 us
    all_to_all x1, starting transfers between devices, on_device(): lax.all_to_all(jnp.stack(jnp.split(out_weight, lax.axis_size(('head', 'su...  4.96 us
    another operation x1, local copies, waits for them, and re-layouts, on_device(): jnp.stack(jnp.split(out_weight, lax.axis_size(('head', 'sub')), axis=1))  2.68 us
    another operation x1, other arithmetic, on_device(): jnp.stack(jnp.split(out_weight, lax.axis_size(('head', 'sub')), axis=1))  2.27 us
    reduce_sum x2, other arithmetic, grouped_project(): return jnp.sum(partial_value, axis=0).astype(jnp.bfloat16)  2.06 us
  transfers between devices with their start and end apart: 1, of which 0 were waited for; matrix products, arithmetic and copies ran while one was open for 9% of the time, Pallas kernels for 0%

profile of v1, /device:TPU:0, one launch (start us, length us, event | category | flops | bytes accessed | tf_op | source)
XLA Modules:
  0.0 83.3 jit_solution(1832997538982441359)
XLA Ops:
  0.6 2.7 %slice_bitcast_fusion.3 = (bf16[1,512,1024]{2,1,0:T(8,128)(2,1)S(1)}, bf16[1,512,1024]{2,1,0:T(8,128)(2,1)S(1)}, bf16[1,512,1024]{2,1,0:T(8,128)(2,1)S(1)}, bf16[1,512,1024]{2,1,0:T(8,128)(2,1)S(1)}) fusion(bf16[512,4096]{1,0:T(8,128)(2,1)} %param.21), kind=kLoop, calls=%fused_computation.18 | loop fusion | bytes 8388608 | tf_op jit(solution)/shard_map/stack | solution.py:63
  3.3 2.3 %pad_maximum_fusion = bf16[4,512,1024]{2,1,0:T(8,128)(2,1)} fusion(bf16[1,512,1024]{2,1,0:T(8,128)(2,1)S(1)} %get-tuple-element.36, bf16[1,512,1024]{2,1,0:T(8,128)(2,1)S(1)} %get-tuple-element.37, bf16[1,512,1024]{2,1,0:T(8,128)(2,1)S(1)} %get-tuple-element.35, bf16[1,512,1024]{2,1,0:T(8,128)(2,1)S(1)} %get-tuple-element.34), kind=kLoop, calls=%fused_computation.1 | loop fusion | flops 6291456 | bytes 8388608 | tf_op jit(solution)/shard_map/stack | solution.py:63
  5.6 5.0 %all-to-all-start = ((bf16[4,512,1024]{2,1,0:T(8,128)(2,1)}), bf16[4,512,1024]{2,1,0:T(8,128)(2,1)}, u32[]{:S(2)}, u32[]{:S(2)}) async-start(bf16[4,512,1024]{2,1,0:T(8,128)(2,1)} %pad_maximum_fusion), calls=%async_computation | async-start | bytes 8388608 | tf_op jit(solution)/shard_map/all_to_all | solution.py:62
  10.7 1.1 %convolution_convert_fusion.2 = bf16[4,128,128]{2,1,0:T(8,128)(2,1)S(1)} fusion(f32[192,512]{1,0:T(8,128)S(1)} %copy-done.2, f32[192,512]{1,0:T(8,128)S(1)} %copy-done), kind=kOutput, calls=%fused_computation.14 | convolution fusion | flops 151060480 | bytes 917504 | tf_op jit(solution)/shard_map/thd,the->hde/dot_general | solution.py:74
  11.8 17.9 %all-gather = bf16[16,128,128]{2,1,0:T(8,128)(2,1)S(1)} all-gather(bf16[4,128,128]{2,1,0:T(8,128)(2,1)S(1)} %convolution_convert_fusion.2), channel_id=2, replica_groups=mesh['grp'=2,'seq'=4,'head'=2,'sub'=2] {'seq'}, dimensions={0}, use_global_device_ids=true | all-gather | bytes 655360 | tf_op jit(solution)/shard_map/all_gather | solution.py:12
  29.7 0.1 fusion.29
  29.8 0.5 convolution_multiply_fusion.1
  30.4 0.1 compare_convert_fusion.1
  30.4 1.9 %fusion = f32[2,4,128,128]{3,2,1,0:T(8,128)S(1)} fusion(f32[192,4,128]{2,0,1:T(8,128)S(1)} %copy_bitcast_fusion, f32[192,2]{0,1:T(2,128)S(1)} %fusion.29, f32[4,128,128]{2,1,0:T(8,128)S(1)} %get-tuple-element.25, f32[192,512]{1,0:T(8,128)S(1)} %copy-done.2), kind=kOutput, calls=%fused_computation.6 | convolution fusion | flops 302317568 | bytes 1574400 | tf_op jit(solution)/shard_map/ot,thd,the->ohde/dot_general | solution.py:83
  32.4 0.6 convolution_bitcast_fusion.3
  32.9 0.5 multiply_reduce_fusion.1
  33.5 0.2 multiply_convert_fusion.1
  33.6 0.1 copy.45
  33.8 29.2 %all_gather.15 = bf16[128,2048]{1,0:T(8,128)(2,1)S(1)} all-gather(bf16[128,512]{1,0:T(8,128)(2,1)S(1)} %bitcast.135), channel_id=1, replica_groups=mesh['grp'=2,'seq'=4,'head'=2,'sub'=2] {'head','sub'}, dimensions={1}, use_global_device_ids=true | all-gather | bytes 655360 | tf_op jit(solution)/shard_map/all_gather | solution.py:101
  63.0 0.3 copy.46
  63.3 0.5 convolution_bitcast_fusion.1
  63.8 0.8 convolution_multiply_fusion
  64.6 1.0 %multiply_reduce_fusion = (f32[192,4]{0,1:T(4,128)S(1)}, f32[192,4,128]{2,0,1:T(8,128)S(1)}) fusion(f32[192,4,128]{2,0,1:T(8,128)S(1)} %convolution_bitcast_fusion.1, f32[4,192,192]{2,1,0:T(8,128)S(1)} %convolution_multiply_fusion, f32[192,512]{1,0:T(8,128)S(1)} %copy-done.2), kind=kOutput, calls=%fused_computation.32 | convolution fusion | flops 226786560 | bytes 1772544 | tf_op jit(solution)/shard_map/hts,she->the/dot_general | solution.py:78
  65.6 0.2 copy_bitcast_fusion.1
  65.8 9.2 %all_gather.14 = bf16[192,2048]{1,0:T(8,128)(2,1)} all-gather(bf16[192,512]{1,0:T(8,128)(2,1)S(1)} %copy_bitcast_fusion.1), channel_id=1, replica_groups=mesh['grp'=2,'seq'=4,'head'=2,'sub'=2] {'head','sub'}, dimensions={1}, use_global_device_ids=true | all-gather | bytes 983040 | tf_op jit(solution)/shard_map/all_gather | solution.py:100
  75.0 3.0 %convolution_convert_fusion.1 = bf16[4,128,1024]{2,1,0:T(8,128)(2,1)S(1)} fusion(bf16[128,4,512]{0,2,1:T(8,128)(2,1)S(1)} %bitcast.133, bf16[4,512,1024]{2,1,0:T(8,128)(2,1)} %all-to-all-done), kind=kOutput, calls=%fused_computation.3 | convolution fusion | flops 537395200 | bytes 5767168 | tf_op jit(solution)/shard_map/rgk,gkd->grd/dot_general | solution.py:36
  78.0 3.2 %convolution_convert_fusion = bf16[4,192,1024]{2,1,0:T(8,128)(2,1)S(1)} fusion(bf16[4,512,1024]{2,1,0:T(8,128)(2,1)} %all-to-all-done, bf16[24,4,8,512]{3,2,1,0:T(8,128)(2,1)S(1)} %bitcast.132), kind=kOutput, calls=%fused_computation.2 | convolution fusion | flops 806092800 | bytes 6553600 | tf_op jit(solution)/shard_map/rgk,gkd->grd/dot_general | solution.py:36
  81.2 0.9 %reduce_sum.45 = bf16[128,1024]{1,0:T(8,128)(2,1)} reduce(bf16[4,128,1024]{2,1,0:T(8,128)(2,1)S(1)} %convolution_convert_fusion.1, bf16[]{:T(256)} %constant.28.clone.1), dimensions={0}, to_apply=%region_5.6 | reduce | flops 393216 | bytes 1310722 | tf_op jit(solution)/shard_map/reduce_sum | solution.py:40
  82.2 1.1 %reduce_sum.43 = bf16[192,1024]{1,0:T(8,128)(2,1)} reduce(bf16[4,192,1024]{2,1,0:T(8,128)(2,1)S(1)} %convolution_convert_fusion, bf16[]{:T(256)} %constant.28.clone.1), dimensions={0}, to_apply=%region_3.4 | reduce | flops 589824 | bytes 1966082 | tf_op jit(solution)/shard_map/reduce_sum | solution.py:40
  (29 shorter events, 0.2 us)
Async XLA Ops:
  0.6 10.0 %copy-start = (f32[192,512]{1,0:T(8,128)S(1)}, f32[192,512]{1,0:T(8,128)}, u32[]{:S(2)}) copy-start(f32[192,512]{1,0:T(8,128)} %param.13) | copy-start | bytes 1179652
  5.6 5.1 %copy-start.2 = (f32[192,512]{1,0:T(8,128)S(1)}, f32[192,512]{1,0:T(8,128)}, u32[]{:S(2)}) copy-start(f32[192,512]{1,0:T(8,128)} %param.14) | copy-start | bytes 1179652
  5.6 69.4 %all-to-all-start = ((bf16[4,512,1024]{2,1,0:T(8,128)(2,1)}), bf16[4,512,1024]{2,1,0:T(8,128)(2,1)}, u32[]{:S(2)}, u32[]{:S(2)}) async-start(bf16[4,512,1024]{2,1,0:T(8,128)(2,1)} %pad_maximum_fusion), calls=%async_computation | async-start | bytes 8388608 | tf_op jit(solution)/shard_map/all_to_all | solution.py:62
  10.6 19.1 %copy-start.8 = (s32[2]{0:T(128)S(1)}, s32[2]{0:T(128)}, u32[]{:S(2)}) copy-start(s32[2]{0:T(128)} %param.18) | copy-start | bytes 28
  10.6 19.2 %copy-start.4 = (f32[2,64,512]{2,1,0:T(8,128)S(1)}, f32[2,64,512]{2,1,0:T(8,128)}, u32[]{:S(2)}) copy-start(f32[2,64,512]{2,1,0:T(8,128)} %param.15) | copy-start | bytes 786436
  10.6 19.2 %copy-start.5 = (f32[2,64,512]{2,1,0:T(8,128)S(1)}, f32[2,64,512]{2,1,0:T(8,128)}, u32[]{:S(2)}) copy-start(f32[2,64,512]{2,1,0:T(8,128)} %param.16) | copy-start | bytes 786436
  10.6 19.7 %copy-start.9 = (s32[2]{0:T(128)S(1)}, s32[2]{0:T(128)}, u32[]{:S(2)}) copy-start(s32[2]{0:T(128)} %param.19) | copy-start | bytes 28
  10.7 22.2 %copy-start.6 = (f32[2,64,512]{2,1,0:T(8,128)S(1)}, f32[2,64,512]{2,1,0:T(8,128)}, u32[]{:S(2)}) copy-start(f32[2,64,512]{2,1,0:T(8,128)} %param.17) | copy-start | bytes 786436
  29.7 3.8 %copy-start.7 = (f32[512]{0:T(512)S(1)}, f32[512]{0:T(512)}, u32[]{:S(2)}) copy-start(f32[512]{0:T(512)} %param.20) | copy-start | bytes 6148
  29.7 33.6 %copy-start.3 = (f32[192,512]{1,0:T(8,128)S(1)}, f32[192,512]{1,0:T(8,128)}, u32[]{:S(2)}) copy-start(f32[192,512]{1,0:T(8,128)} %param.12) | copy-start | bytes 1179652
  75.0 3.0 %copy-start.1 = (bf16[192,2048]{1,0:T(8,128)(2,1)S(1)}, bf16[192,2048]{1,0:T(8,128)(2,1)}, u32[]{:S(2)}) copy-start(bf16[192,2048]{1,0:T(8,128)(2,1)} %all_gather.14) | copy-start | bytes 2359300
